TPU v7x, 256 devices: a whole 4x4x8 slice. The times are simulated.
256 devices in a mesh: dp: 8 (over y, core), ctx: 32 (over x, z).
Axes of the slice: x: 4, y: 4, z: 8, core: 2. Of those that a mesh axis runs over, the one named last changes fastest.
Arguments:
- queries: bfloat16 [8, 8192, 2560], P('dp', 'ctx'), may hold values from -120 to 120
- global_keys: bfloat16 [8, 8192, 512], P('dp', 'ctx'), may hold values from -5 to 5
- global_values: bfloat16 [8, 8192, 512], P('dp', 'ctx'), may hold values from -6 to 6
- out_grad: bfloat16 [8, 8192, 2560], P('dp', 'ctx'), may hold values from -6 to 6
- query_gain: float32 [2560], replicated, may hold values from 0.5 to 1.5
- doc_start: int32 [8, 64], P('dp', 'ctx'), may hold values from 0 to 63, as said below
Outputs:
- attn_out: bfloat16 [8, 8192, 2560], P('dp', 'ctx')
- query_grad: bfloat16 [8, 8192, 2560], P('dp', 'ctx')
- key_grad: bfloat16 [8, 8192, 512], P('dp', 'ctx')
- value_grad: bfloat16 [8, 8192, 512], P('dp', 'ctx')
- gain_grad: float32 [2560], replicated
Inputs may be any that keep to these rules, and one draw needn't show every extreme that they name: doc_start[g, b] is the first block of block b's document: it is at most b and at least b - 6, never falls along b, and equals b where a document begins; every slab has a document of exactly 7 blocks.
All inputs are finite; a program needn't handle non-finite values.
Results may differ from a plain program's by a relative error of at most 0.017.
The roundings to bfloat16 on the way count: a program that leaves them out, or rounds other values in their place, can miss the bound.
Values may be sent and summed in bfloat16 or wider, within the bound.
No kernel may reach another device: no remote copies, remote signals or barrier semaphores. Data moves between devices by JAX's collectives and lax.ppermute only.
A program may use at most 64 MiB of HBM per device.

v0:
```python
import math
import jax
import jax.numpy as jnp
from jax import lax
from jax.sharding import PartitionSpec as P

HD = 128
BLOCK = 128
REACH = 4


def shifted(value, axis, steps):
    count = lax.axis_size(axis)
    first, last = (max(0, -steps), min(count, count - steps))
    return lax.ppermute(value, axis, [(source, source + steps) for source in range(first, last)])


def head_group(inputs, allowed, factor):
    query_part, key_part, value_part, grad_part = inputs
    scores = (
        jnp.einsum("tgd,wd->gtw", query_part, key_part, preferred_element_type=jnp.float32) * factor
    )
    scores = jnp.where(allowed[None], scores, -jnp.inf)
    row_max = jnp.max(scores, axis=-1, keepdims=True)
    log_total = row_max + jnp.log(jnp.sum(jnp.exp(scores - row_max), axis=-1, keepdims=True))
    weights = jnp.exp(scores - log_total)
    weights_low = weights.astype(jnp.bfloat16)
    result = jnp.einsum(
        "gtw,wd->tgd", weights_low, value_part, preferred_element_type=jnp.float32
    ).astype(jnp.bfloat16)
    inner_sum = jnp.einsum("tgd,tgd->gt", grad_part, result, preferred_element_type=jnp.float32)
    dweights = jnp.einsum("tgd,wd->gtw", grad_part, value_part, preferred_element_type=jnp.float32)
    dscore_low = (weights * (dweights - inner_sum[..., None])).astype(jnp.bfloat16)
    dquery = (
        jnp.einsum("gtw,wd->tgd", dscore_low, key_part, preferred_element_type=jnp.float32) * factor
    )
    dkey = (
        jnp.einsum("gtw,tgd->wd", dscore_low, query_part, preferred_element_type=jnp.float32)
        * factor
    )
    dvalue = jnp.einsum("gtw,tgd->wd", weights_low, grad_part, preferred_element_type=jnp.float32)
    return (result, dquery, dkey, dvalue)


def local(queries, global_keys, global_values, out_grad, query_gain, doc_start):
    row_count = queries.shape[1]
    reach = REACH
    width = reach * row_count
    device = lax.axis_index("ctx")
    query_rows = queries[0]
    key_rows = global_keys[0]
    value_rows = global_values[0]
    grad_rows = out_grad[0]
    kv_count = key_rows.shape[1] // HD
    group_size = query_rows.shape[1] // (kv_count * HD)
    factor = 1.0 / math.sqrt(HD)
    scaled = (query_rows.astype(jnp.float32) * query_gain).astype(jnp.bfloat16)
    key_list = [key_rows]
    value_list = [value_rows]
    for distance in range(1, reach):
        far_keys, far_values = shifted((key_rows, value_rows), "ctx", distance)
        key_list.insert(0, far_keys)
        value_list.insert(0, far_values)
    window_keys = jnp.concatenate(key_list, axis=0)
    window_values = jnp.concatenate(value_list, axis=0)
    first_device = device - (reach - 1)
    query_pos = device * row_count + jnp.arange(row_count, dtype=jnp.int32)
    key_pos = first_device * row_count + jnp.arange(width, dtype=jnp.int32)
    begins = jnp.repeat(doc_start[0], BLOCK) * BLOCK
    allowed = (key_pos[None, :] <= query_pos[:, None]) & (key_pos[None, :] >= begins[:, None])
    query_four = scaled.reshape(row_count, kv_count, group_size, HD).transpose(1, 0, 2, 3)
    grad_four = grad_rows.reshape(row_count, kv_count, group_size, HD).transpose(1, 0, 2, 3)
    key_three = window_keys.reshape(width, kv_count, HD).transpose(1, 0, 2)
    value_three = window_values.reshape(width, kv_count, HD).transpose(1, 0, 2)
    results, dqueries, dkeys, dvalues = lax.map(
        lambda inputs: head_group(inputs, allowed, factor),
        (query_four, key_three, value_three, grad_four),
    )
    attn_out = results.transpose(1, 0, 2, 3).reshape(row_count, -1)
    dscaled = dqueries.transpose(1, 0, 2, 3).reshape(row_count, -1)

    def by_offset(partial_value):
        return partial_value.reshape(kv_count, reach, row_count, HD)[:, ::-1]

    key_offsets = by_offset(dkeys)
    value_offsets = by_offset(dvalues)
    key_total = key_offsets[:, 0]
    value_total = value_offsets[:, 0]
    for distance in range(1, reach):
        got_keys, got_values = shifted(
            (key_offsets[:, distance], value_offsets[:, distance]), "ctx", -distance
        )
        key_total = key_total + got_keys
        value_total = value_total + got_values
    key_grad = key_total.transpose(1, 0, 2).reshape(row_count, -1).astype(jnp.bfloat16)
    value_grad = value_total.transpose(1, 0, 2).reshape(row_count, -1).astype(jnp.bfloat16)
    query_grad = (dscaled * query_gain).astype(jnp.bfloat16)
    gain_term = jnp.sum(dscaled * query_rows.astype(jnp.float32), axis=0)
    gain_grad = lax.psum(gain_term, ("dp", "ctx"))
    return (attn_out[None], query_grad[None], key_grad[None], value_grad[None], gain_grad)


def solution(mesh):
    return jax.shard_map(
        local,
        mesh=mesh,
        in_specs=(
            P("dp", "ctx", None),
            P("dp", "ctx", None),
            P("dp", "ctx", None),
            P("dp", "ctx", None),
            P(),
            P("dp", "ctx"),
        ),
        out_specs=(
            P("dp", "ctx", None),
            P("dp", "ctx", None),
            P("dp", "ctx", None),
            P("dp", "ctx", None),
            P(),
        ),
        check_vma=False,
    )
```

profile of v0, /device:TPU:1, one launch (start us, length us, event | category | flops | bytes accessed | tf_op | source)
XLA Modules:
  0.0 343.3 jit_solution(1276972712751430127)
XLA Ops:
  1.7 5.1 %collective-permute-start.5 = (bf16[256,512]{0,1:T(8,128)(2,1)S(1)}, bf16[256,512]{0,1:T(8,128)(2,1)}, u32[]{:S(2)}, u32[]{:S(2)}) collective-permute-start(bf16[256,512]{0,1:T(8,128)(2,1)S(1)} %bitcast.227), channel_id=1, source_target_pairs={{0,1},{1,2},{2,3},{3,4},{4,5},{5,6},{6,7},{7,8},{8,9},{9,10},{10,1... | collective-permute-start | bytes 786440 | tf_op jit(solution)/shard_map/ppermute | solution.py:15
  6.8 4.9 %collective-permute-start.4 = (bf16[256,512]{0,1:T(8,128)(2,1)S(1)}, bf16[256,512]{0,1:T(8,128)(2,1)}, u32[]{:S(2)}, u32[]{:S(2)}) collective-permute-start(bf16[256,512]{0,1:T(8,128)(2,1)S(1)} %bitcast.228), channel_id=1, source_target_pairs={{0,2},{1,3},{2,4},{3,5},{4,6},{5,7},{6,8},{7,9},{8,10},{9,11},{10,... | collective-permute-start | bytes 786440 | tf_op jit(solution)/shard_map/ppermute | solution.py:15
  11.7 5.7 %collective-permute-start.3 = (bf16[256,512]{0,1:T(8,128)(2,1)S(1)}, bf16[256,512]{0,1:T(8,128)(2,1)}, u32[]{:S(2)}, u32[]{:S(2)}) collective-permute-start(bf16[256,512]{0,1:T(8,128)(2,1)S(1)} %bitcast.229), channel_id=1, source_target_pairs={{0,3},{1,4},{2,5},{3,6},{4,7},{5,8},{6,9},{7,10},{8,11},{9,12},{10... | collective-permute-start | bytes 786440 | tf_op jit(solution)/shard_map/ppermute | solution.py:15
  17.4 2.6 collective-permute-start.2
  20.0 2.3 collective-permute-start.1
  26.5 17.9 %collective-permute-done.2 = bf16[256,512]{1,0:T(8,128)(2,1)S(1)} collective-permute-done((bf16[256,512]{1,0:T(8,128)(2,1)}, bf16[256,512]{1,0:T(8,128)(2,1)S(1)}, u32[]{:S(2)}, u32[]{:S(2)}) %collective-permute-start.2) | collective-permute-done | bytes 262176 | tf_op jit(solution)/shard_map/ppermute | solution.py:15
  44.5 9.5 %collective-permute-start = (bf16[256,512]{1,0:T(8,128)(2,1)S(1)}, bf16[256,512]{1,0:T(8,128)(2,1)}, u32[]{:S(2)}, u32[]{:S(2)}) collective-permute-start(bf16[256,512]{1,0:T(8,128)(2,1)S(1)} %bitcast.240), channel_id=1, source_target_pairs={{0,3},{1,4},{2,5},{3,6},{4,7},{5,8},{6,9},{7,10},{8,11},{9,12},{10... | collective-permute-start | bytes 786440 | tf_op jit(solution)/shard_map/ppermute | solution.py:15
  54.1 2.5 copy.42
  63.4 68.0 %while.17 = (s32[]{:T(128)}, bf16[4,256,5,128]{1,3,2,0:T(8,128)(2,1)}, f32[4,256,5,128]{1,3,2,0:T(8,128)}, f32[4,1024,128]{2,1,0:T(8,128)}, f32[4,1024,128]{2,1,...) while((s32[]{:T(128)}, ...), condition=%wide.region_3.4_spmd.clone, body=%wide.region_0.3_spmd.clone.sunk | while | flops 2042689024 | bytes 49229988 | solution.py:75
  70.7 3.1 fusion.75
  73.8 2.6 fusion.72
  78.1 2.3 fusion.73
  87.7 3.1 fusion.75
  90.8 2.6 fusion.72
  95.1 2.3 fusion.73
  104.7 3.1 fusion.75
  107.8 2.6 fusion.72
  112.1 2.3 fusion.73
  121.7 3.1 fusion.75
  124.8 2.6 fusion.72
  129.1 2.3 fusion.73
  145.0 33.2 %collective-permute-done.11 = f32[4,256,128]{2,0,1:T(4,128)S(1)} collective-permute-done((f32[4,256,128]{2,0,1:T(4,128)S(1)}, f32[4,256,128]{2,0,1:T(4,128)S(1)}, u32[]{:S(2)}, u32[]{:S(2)}) %collective-permute-start.11) | collective-permute-done | bytes 524320 | tf_op jit(solution)/shard_map/ppermute | solution.py:15
  180.0 2.4 copy.54
  184.0 153.9 %psum.7 = f32[2560]{0:T(1024)} all-reduce(f32[2560]{0:T(1024)S(1)} %reduce_sum.21), channel_id=1, replica_groups=mesh['dp'=8,'ctx'=32] {'dp','ctx'}, use_global_device_ids=true, to_apply=%region_5.6 | all-reduce | flops 2560 | bytes 20480 | tf_op jit(solution)/shard_map/psum | solution.py:99
  (122 shorter events, 69.8 us)
Async XLA Ops:
  1.7 57.2 %collective-permute-start.5 = (bf16[256,512]{0,1:T(8,128)(2,1)S(1)}, bf16[256,512]{0,1:T(8,128)(2,1)}, u32[]{:S(2)}, u32[]{:S(2)}) collective-permute-start(bf16[256,512]{0,1:T(8,128)(2,1)S(1)} %bitcast.227), channel_id=1, source_target_pairs={{0,1},{1,2},{2,3},{3,4},{4,5},{5,6},{6,7},{7,8},{8,9},{9,10},{10,1... | collective-permute-start | bytes 786440 | tf_op jit(solution)/shard_map/ppermute | solution.py:15
  6.8 52.1 %collective-permute-start.4 = (bf16[256,512]{0,1:T(8,128)(2,1)S(1)}, bf16[256,512]{0,1:T(8,128)(2,1)}, u32[]{:S(2)}, u32[]{:S(2)}) collective-permute-start(bf16[256,512]{0,1:T(8,128)(2,1)S(1)} %bitcast.228), channel_id=1, source_target_pairs={{0,2},{1,3},{2,4},{3,5},{4,6},{5,7},{6,8},{7,9},{8,10},{9,11},{10,... | collective-permute-start | bytes 786440 | tf_op jit(solution)/shard_map/ppermute | solution.py:15
  11.7 47.2 %collective-permute-start.3 = (bf16[256,512]{0,1:T(8,128)(2,1)S(1)}, bf16[256,512]{0,1:T(8,128)(2,1)}, u32[]{:S(2)}, u32[]{:S(2)}) collective-permute-start(bf16[256,512]{0,1:T(8,128)(2,1)S(1)} %bitcast.229), channel_id=1, source_target_pairs={{0,3},{1,4},{2,5},{3,6},{4,7},{5,8},{6,9},{7,10},{8,11},{9,12},{10... | collective-permute-start | bytes 786440 | tf_op jit(solution)/shard_map/ppermute | solution.py:15
  17.4 27.1 %collective-permute-start.2 = (bf16[256,512]{1,0:T(8,128)(2,1)}, bf16[256,512]{1,0:T(8,128)(2,1)S(1)}, u32[]{:S(2)}, u32[]{:S(2)}) collective-permute-start(bf16[256,512]{1,0:T(8,128)(2,1)} %bitcast.238), channel_id=1, source_target_pairs={{0,1},{1,2},{2,3},{3,4},{4,5},{5,6},{6,7},{7,8},{8,9},{9,10},{10,1... | collective-permute-start | bytes 786440 | tf_op jit(solution)/shard_map/ppermute | solution.py:15
  20.0 37.7 %collective-permute-start.1 = (bf16[256,512]{1,0:T(8,128)(2,1)}, bf16[256,512]{1,0:T(8,128)(2,1)}, u32[]{:S(2)}, u32[]{:S(2)}) collective-permute-start(bf16[256,512]{1,0:T(8,128)(2,1)} %bitcast.239), channel_id=1, source_target_pairs={{0,2},{1,3},{2,4},{3,5},{4,6},{5,7},{6,8},{7,9},{8,10},{9,11},{10,... | collective-permute-start | bytes 786440 | tf_op jit(solution)/shard_map/ppermute | solution.py:15
  24.7 31.9 %copy-start = (f32[1,256,2560]{1,2,0:T(8,128)}, f32[1,256,2560]{1,2,0:T(8,128)S(1)}, u32[]{:S(2)}) copy-start(f32[1,256,2560]{1,2,0:T(8,128)S(1)} %copy.41) | copy-start | bytes 7864324
  24.7 1.8 copy-start.10
  24.7 19.7 %copy-start.7 = (bf16[1,256,512]{2,1,0:T(8,128)(2,1)S(1)}, bf16[1,256,512]{2,1,0:T(8,128)(2,1)}, u32[]{:S(2)}) copy-start(bf16[1,256,512]{2,1,0:T(8,128)(2,1)} %param.10) | copy-start | bytes 786436
  44.5 9.5 %copy-start.8 = (bf16[256,512]{1,0:T(8,128)(2,1)}, bf16[256,512]{1,0:T(8,128)(2,1)S(1)}, u32[]{:S(2)}) copy-start(bf16[256,512]{1,0:T(8,128)(2,1)S(1)} %collective-permute-done.2) | copy-start | bytes 786436
  44.5 16.7 %collective-permute-start = (bf16[256,512]{1,0:T(8,128)(2,1)S(1)}, bf16[256,512]{1,0:T(8,128)(2,1)}, u32[]{:S(2)}, u32[]{:S(2)}) collective-permute-start(bf16[256,512]{1,0:T(8,128)(2,1)S(1)} %bitcast.240), channel_id=1, source_target_pairs={{0,3},{1,4},{2,5},{3,6},{4,7},{5,8},{6,9},{7,10},{8,11},{9,12},{10... | collective-permute-start | bytes 786440 | tf_op jit(solution)/shard_map/ppermute | solution.py:15
  57.7 5.7 %copy-start.2 = (bf16[4,256,5,128]{1,3,2,0:T(8,128)(2,1)S(1)}, bf16[4,256,5,128]{1,3,2,0:T(8,128)(2,1)}, u32[]{:S(2)}) copy-start(bf16[4,256,5,128]{1,3,2,0:T(8,128)(2,1)} %fusion.35) | copy-start | bytes 3932164
  67.1 1.2 copy-start.5
  101.1 1.2 copy-start.5
  133.1 6.1 %copy-start.3 = (f32[4,256,5,128]{1,3,2,0:T(8,128)S(1)}, f32[4,256,5,128]{1,3,2,0:T(8,128)}, u32[]{:S(2)}) copy-start(f32[4,256,5,128]{1,3,2,0:T(8,128)} %get-tuple-element.61) | copy-start | bytes 7864324
  133.1 6.1 %copy-start.9 = (f32[2560]{0:T(1024)S(1)}, f32[2560]{0:T(1024)}, u32[]{:S(2)}) copy-start(f32[2560]{0:T(1024)} %param.12) | copy-start | bytes 30724
  134.6 5.0 %copy-start.4 = (f32[4,1024,128]{2,1,0:T(8,128)S(1)}, f32[4,1024,128]{2,1,0:T(8,128)}, u32[]{:S(2)}) copy-start(f32[4,1024,128]{2,1,0:T(8,128)} %get-tuple-element.62) | copy-start | bytes 6291460
  134.9 43.2 %collective-permute-start.11 = (f32[4,256,128]{2,0,1:T(4,128)S(1)}, f32[4,256,128]{2,0,1:T(4,128)S(1)}, u32[]{:S(2)}, u32[]{:S(2)}) collective-permute-start(f32[4,256,128]{2,0,1:T(4,128)S(1)} %bitcast.237), channel_id=1, source_target_pairs={{3,0},{4,1},{5,2},{6,3},{7,4},{8,5},{9,6},{10,7},{11,8},{12,9},{13... | collective-permute-start | bytes 1572872 | tf_op jit(solution)/shard_map/ppermute | solution.py:15
  136.4 201.5 %collective-permute-start.9 = (f32[4,256,128]{2,0,1:T(4,128)}, f32[4,256,128]{2,0,1:T(4,128)}, u32[]{:S(2)}, u32[]{:S(2)}) collective-permute-start(f32[4,256,128]{2,0,1:T(4,128)} %bitcast.170), channel_id=1, source_target_pairs={{1,0},{2,1},{3,2},{4,3},{5,4},{6,5},{7,6},{8,7},{9,8},{10,9},{11,1... | collective-permute-start | bytes 1572872 | tf_op jit(solution)/shard_map/ppermute | solution.py:15
  137.7 200.2 %collective-permute-start.10 = (f32[4,256,128]{2,0,1:T(4,128)S(1)}, f32[4,256,128]{2,0,1:T(4,128)}, u32[]{:S(2)}, u32[]{:S(2)}) collective-permute-start(f32[4,256,128]{2,0,1:T(4,128)S(1)} %bitcast.235), channel_id=1, source_target_pairs={{2,0},{3,1},{4,2},{5,3},{6,4},{7,5},{8,6},{9,7},{10,8},{11,9},{12,... | collective-permute-start | bytes 1572872 | tf_op jit(solution)/shard_map/ppermute | solution.py:15
  139.8 39.7 %copy-start.1 = (f32[1,256,2560]{1,2,0:T(8,128)S(1)}, f32[1,256,2560]{1,2,0:T(8,128)}, u32[]{:S(2)}) copy-start(f32[1,256,2560]{1,2,0:T(8,128)} %copy-done) | copy-start | bytes 7864324
  142.4 198.2 %collective-permute-start.8 = (f32[4,256,128]{2,0,1:T(4,128)}, f32[4,256,128]{2,0,1:T(4,128)}, u32[]{:S(2)}, u32[]{:S(2)}) collective-permute-start(f32[4,256,128]{2,0,1:T(4,128)} %bitcast.171), channel_id=1, source_target_pairs={{3,0},{4,1},{5,2},{6,3},{7,4},{8,5},{9,6},{10,7},{11,8},{12,9},{13... | collective-permute-start | bytes 1572872 | tf_op jit(solution)/shard_map/ppermute | solution.py:15
  143.7 196.9 %collective-permute-start.6 = (f32[4,256,128]{2,0,1:T(4,128)}, f32[4,256,128]{2,0,1:T(4,128)}, u32[]{:S(2)}, u32[]{:S(2)}) collective-permute-start(f32[4,256,128]{2,0,1:T(4,128)} %bitcast.173), channel_id=1, source_target_pairs={{1,0},{2,1},{3,2},{4,3},{5,4},{6,5},{7,6},{8,7},{9,8},{10,9},{11,1... | collective-permute-start | bytes 1572872 | tf_op jit(solution)/shard_map/ppermute | solution.py:15
  178.2 1.3 copy-start.6
  178.2 162.4 %collective-permute-start.7 = (f32[4,256,128]{2,0,1:T(4,128)S(1)}, f32[4,256,128]{2,0,1:T(4,128)}, u32[]{:S(2)}, u32[]{:S(2)}) collective-permute-start(f32[4,256,128]{2,0,1:T(4,128)S(1)} %bitcast.236), channel_id=1, source_target_pairs={{2,0},{3,1},{4,2},{5,3},{6,4},{7,5},{8,6},{9,7},{10,8},{11,9},{12,... | collective-permute-start | bytes 1572872 | tf_op jit(solution)/shard_map/ppermute | solution.py:15
  (2 other events, 2.5 us)
where the time goes:
time: 345 us; the launch traced here: 343 us
  blocking collectives  154 us (45%)
  matrix products  55.5 us (16%)
  waiting for transfers between devices  51.1 us (15%)
  starting transfers between devices  38.2 us (11%)
  local copies, waits for them, and re-layouts  27.5 us (8%)
  other arithmetic  15.8 us (5%)
    psum x1, blocking collectives, local(): gain_grad = lax.psum(gain_term, ('dp', 'ctx'))  154 us
    ppermute x12, waiting for transfers between devices, shifted(): lax.ppermute(value, axis, [(source, source + steps) for source in range(f...  51.1 us
    ppermute x12, starting transfers between devices, shifted(): lax.ppermute(value, axis, [(source, source + steps) for source in range(f...  38.2 us
    dot_general x4, matrix products, head_group(): jnp.einsum('gtw,tgd->wd', weights_low, grad_part, preferred_element_type=...  12.5 us
    unnamed x31, local copies, waits for them, and re-layouts  12.2 us
    dot_general x4, matrix products, head_group(): jnp.einsum('tgd,wd->gtw', grad_part, value_part, preferred_element_type=j...  10.4 us
    dot_general x4, matrix products, head_group(): jnp.einsum('gtw,wd->tgd', dscore_low, key_part, preferred_element_type=jn...  9.25 us
    dot_general x4, matrix products, head_group(): jnp.einsum('gtw,wd->tgd', weights_low, value_part, preferred_element_type...  8.8 us
  transfers between devices with their start and end apart: 12, of which 2 were waited for; matrix products, arithmetic and copies ran while one was open for 6% of the time, Pallas kernels for 0%

commit v1 on v0

--- a/solution.py
+++ b/solution.py
@@ -43,6 +43,10 @@
 
 
 def local(queries, global_keys, global_values, out_grad, query_gain, doc_start):
+
+    def supply_all_page_up(sheet):
+        return jnp.sum(lax.all_gather(sheet, ("dp", "ctx")), 0)
+
     row_count = queries.shape[1]
     reach = REACH
     width = reach * row_count
@@ -96,7 +100,7 @@
     value_grad = value_total.transpose(1, 0, 2).reshape(row_count, -1).astype(jnp.bfloat16)
     query_grad = (dscaled * query_gain).astype(jnp.bfloat16)
     gain_term = jnp.sum(dscaled * query_rows.astype(jnp.float32), axis=0)
-    gain_grad = lax.psum(gain_term, ("dp", "ctx"))
+    gain_grad = supply_all_page_up(gain_term)
     return (attn_out[None], query_grad[None], key_grad[None], value_grad[None], gain_grad)
 
 

time: 345 us -> 333 us (0.965)
  the two profiles are of different devices: /device:TPU:1 before, /device:TPU:51 now
where the time goes in v1:
time: 333 us; the launch traced here: 332 us
  waiting for transfers between devices  167 us (50%)
  matrix products  55.5 us (17%)
  starting transfers between devices  44.5 us (13%)
  local copies, waits for them, and re-layouts  27.4 us (8%)
  other arithmetic  22.3 us (7%)
  between operations  14.4 us (4%)
    ppermute x12, waiting for transfers between devices, shifted(): lax.ppermute(value, axis, [(source, source + steps) for source in range(f...  135 us
    ppermute x12, starting transfers between devices, shifted(): lax.ppermute(value, axis, [(source, source + steps) for source in range(f...  44.4 us
    all_gather x1, waiting for transfers between devices, supply_all_page_up(): return jnp.sum(lax.all_gather(sheet, ('dp', 'ctx')), 0)  32 us
    unnamed x32, local copies, waits for them, and re-layouts  13.6 us
    dot_general x4, matrix products, head_group(): jnp.einsum('gtw,tgd->wd', weights_low, grad_part, preferred_element_type=...  12.5 us
    dot_general x4, matrix products, head_group(): jnp.einsum('tgd,wd->gtw', grad_part, value_part, preferred_element_type=j...  10.4 us
    dot_general x4, matrix products, head_group(): jnp.einsum('gtw,wd->tgd', dscore_low, key_part, preferred_element_type=jn...  9.26 us
    dot_general x4, matrix products, head_group(): jnp.einsum('gtw,wd->tgd', weights_low, value_part, preferred_element_type...  8.8 us
  transfers between devices with their start and end apart: 13, of which 9 were waited for; matrix products, arithmetic and copies ran while one was open for 8% of the time, Pallas kernels for 0%

profile of v1, /device:TPU:51, one launch (start us, length us, event | category | flops | bytes accessed | tf_op | source)
XLA Modules:
  0.0 331.5 jit_solution(278309342295783716)
XLA Ops:
  8.3 3.5 %collective-permute-start.5 = (bf16[256,512]{0,1:T(8,128)(2,1)S(1)}, bf16[256,512]{0,1:T(8,128)(2,1)}, u32[]{:S(2)}, u32[]{:S(2)}) collective-permute-start(bf16[256,512]{0,1:T(8,128)(2,1)S(1)} %bitcast.227), channel_id=1, source_target_pairs={{0,1},{1,2},{2,3},{3,4},{4,5},{5,6},{6,7},{7,8},{8,9},{9,10},{10,1... | collective-permute-start | bytes 786440 | tf_op jit(solution)/shard_map/ppermute | solution.py:15
  11.9 6.1 %collective-permute-start.4 = (bf16[256,512]{0,1:T(8,128)(2,1)S(1)}, bf16[256,512]{0,1:T(8,128)(2,1)}, u32[]{:S(2)}, u32[]{:S(2)}) collective-permute-start(bf16[256,512]{0,1:T(8,128)(2,1)S(1)} %bitcast.228), channel_id=1, source_target_pairs={{0,2},{1,3},{2,4},{3,5},{4,6},{5,7},{6,8},{7,9},{8,10},{9,11},{10,... | collective-permute-start | bytes 786440 | tf_op jit(solution)/shard_map/ppermute | solution.py:15
  18.0 3.6 %collective-permute-start.3 = (bf16[256,512]{0,1:T(8,128)(2,1)S(1)}, bf16[256,512]{0,1:T(8,128)(2,1)}, u32[]{:S(2)}, u32[]{:S(2)}) collective-permute-start(bf16[256,512]{0,1:T(8,128)(2,1)S(1)} %bitcast.229), channel_id=1, source_target_pairs={{0,3},{1,4},{2,5},{3,6},{4,7},{5,8},{6,9},{7,10},{8,11},{9,12},{10... | collective-permute-start | bytes 786440 | tf_op jit(solution)/shard_map/ppermute | solution.py:15
  23.5 2.9 collective-permute-start.1
  30.5 21.2 %collective-permute-done.2 = bf16[256,512]{1,0:T(8,128)(2,1)S(1)} collective-permute-done((bf16[256,512]{1,0:T(8,128)(2,1)}, bf16[256,512]{1,0:T(8,128)(2,1)S(1)}, u32[]{:S(2)}, u32[]{:S(2)}) %collective-permute-start.2) | collective-permute-done | bytes 262176 | tf_op jit(solution)/shard_map/ppermute | solution.py:15
  51.7 11.5 %collective-permute-start = (bf16[256,512]{1,0:T(8,128)(2,1)S(1)}, bf16[256,512]{1,0:T(8,128)(2,1)}, u32[]{:S(2)}, u32[]{:S(2)}) collective-permute-start(bf16[256,512]{1,0:T(8,128)(2,1)S(1)} %bitcast.239), channel_id=1, source_target_pairs={{0,3},{1,4},{2,5},{3,6},{4,7},{5,8},{6,9},{7,10},{8,11},{9,12},{10... | collective-permute-start | bytes 786440 | tf_op jit(solution)/shard_map/ppermute | solution.py:15
  70.5 13.6 %collective-permute-done = bf16[256,512]{1,0:T(8,128)(2,1)} collective-permute-done((bf16[256,512]{1,0:T(8,128)(2,1)S(1)}, bf16[256,512]{1,0:T(8,128)(2,1)}, u32[]{:S(2)}, u32[]{:S(2)}) %collective-permute-start) | collective-permute-done | bytes 262176 | tf_op jit(solution)/shard_map/ppermute | solution.py:15
  86.3 68.1 %while.17 = (s32[]{:T(128)}, bf16[4,256,5,128]{1,3,2,0:T(8,128)(2,1)}, f32[4,256,5,128]{1,3,2,0:T(8,128)}, f32[4,1024,128]{2,1,0:T(8,128)}, f32[4,1024,128]{2,1,...) while((s32[]{:T(128)}, ...), condition=%wide.region_3.4_spmd.clone, body=%wide.region_0.3_spmd.clone.sunk | while | flops 2042689024 | bytes 49229988 | solution.py:79
  93.6 3.1 fusion.75
  110.6 3.2 fusion.75
  113.8 2.6 fusion.72
  127.7 3.1 fusion.75
  130.8 2.6 fusion.72
  144.7 3.1 fusion.75
  154.4 3.1 fusion.34
  158.7 5.0 %collective-permute-start.11 = (f32[4,256,128]{2,0,1:T(4,128)S(1)}, f32[4,256,128]{2,0,1:T(4,128)S(1)}, u32[]{:S(2)}, u32[]{:S(2)}) collective-permute-start(f32[4,256,128]{2,0,1:T(4,128)S(1)} %bitcast.236), channel_id=1, source_target_pairs={{3,0},{4,1},{5,2},{6,3},{7,4},{8,5},{9,6},{10,7},{11,8},{12,9},{13... | collective-permute-start | bytes 1572872 | tf_op jit(solution)/shard_map/ppermute | solution.py:15
  176.9 21.6 %collective-permute-done.11 = f32[4,256,128]{2,0,1:T(4,128)S(1)} collective-permute-done((f32[4,256,128]{2,0,1:T(4,128)S(1)}, f32[4,256,128]{2,0,1:T(4,128)S(1)}, u32[]{:S(2)}, u32[]{:S(2)}) %collective-permute-start.11) | collective-permute-done | bytes 524320 | tf_op jit(solution)/shard_map/ppermute | solution.py:15
  204.8 5.1 %collective-permute-done.9 = f32[4,256,128]{2,0,1:T(4,128)} collective-permute-done((f32[4,256,128]{2,0,1:T(4,128)}, f32[4,256,128]{2,0,1:T(4,128)}, u32[]{:S(2)}, u32[]{:S(2)}) %collective-permute-start.9) | collective-permute-done | bytes 524320 | tf_op jit(solution)/shard_map/ppermute | solution.py:15
  209.9 9.2 %collective-permute-done.10 = f32[4,256,128]{2,0,1:T(4,128)} collective-permute-done((f32[4,256,128]{2,0,1:T(4,128)}, f32[4,256,128]{2,0,1:T(4,128)}, u32[]{:S(2)}, u32[]{:S(2)}) %collective-permute-start.10) | collective-permute-done | bytes 524320 | tf_op jit(solution)/shard_map/ppermute | solution.py:15
  221.7 45.2 %collective-permute-done.8 = f32[4,256,128]{2,0,1:T(4,128)} collective-permute-done((f32[4,256,128]{2,0,1:T(4,128)}, f32[4,256,128]{2,0,1:T(4,128)}, u32[]{:S(2)}, u32[]{:S(2)}) %collective-permute-start.8) | collective-permute-done | bytes 524320 | tf_op jit(solution)/shard_map/ppermute | solution.py:15
  266.9 11.3 %collective-permute-done.6 = f32[4,256,128]{2,0,1:T(4,128)} collective-permute-done((f32[4,256,128]{2,0,1:T(4,128)}, f32[4,256,128]{2,0,1:T(4,128)}, u32[]{:S(2)}, u32[]{:S(2)}) %collective-permute-start.6) | collective-permute-done | bytes 524320 | tf_op jit(solution)/shard_map/ppermute | solution.py:15
  278.2 8.0 %collective-permute-done.7 = f32[4,256,128]{2,0,1:T(4,128)} collective-permute-done((f32[4,256,128]{2,0,1:T(4,128)S(1)}, f32[4,256,128]{2,0,1:T(4,128)}, u32[]{:S(2)}, u32[]{:S(2)}) %collective-permute-start.7) | collective-permute-done | bytes 524320 | tf_op jit(solution)/shard_map/ppermute | solution.py:15
  288.9 32.0 %all-gather.3.cloned.1.call-done = f32[256,1,2560]{2,1,0:T(1,128)} async-done(((f32[1,1,2560]{2,1,0:T(1,128)}), f32[256,1,2560]{2,1,0:T(1,128)}) %all-gather.3.cloned.1.call-update) | async-done | bytes 2621456 | tf_op jit(solution)/shard_map/all_gather | solution.py:48
  320.9 3.8 %reduce_sum.28 = f32[2560]{0:T(1024)} reduce(f32[256,1,2560]{2,1,0:T(1,128)} %all-gather.3.cloned.1.call-done, f32[]{:T(128)} %constant.11.clone.1), dimensions={0,1}, to_apply=%region_5.6 | reduce | flops 652800 | bytes 2631684 | tf_op jit(solution)/shard_map/reduce_sum | solution.py:48
  (125 shorter events, 92.4 us)
Async XLA Ops:
  7.2 313.7 %all-gather.3.cloned.1.call-start = ((), (), s32[]{:S(2)}) async-start(), calls=%async_computation | async-start | bytes 2631680 | tf_op jit(solution)/shard_map/all_gather | solution.py:48
  8.3 59.9 %collective-permute-start.5 = (bf16[256,512]{0,1:T(8,128)(2,1)S(1)}, bf16[256,512]{0,1:T(8,128)(2,1)}, u32[]{:S(2)}, u32[]{:S(2)}) collective-permute-start(bf16[256,512]{0,1:T(8,128)(2,1)S(1)} %bitcast.227), channel_id=1, source_target_pairs={{0,1},{1,2},{2,3},{3,4},{4,5},{5,6},{6,7},{7,8},{8,9},{9,10},{10,1... | collective-permute-start | bytes 786440 | tf_op jit(solution)/shard_map/ppermute | solution.py:15
  11.9 56.3 %collective-permute-start.4 = (bf16[256,512]{0,1:T(8,128)(2,1)S(1)}, bf16[256,512]{0,1:T(8,128)(2,1)}, u32[]{:S(2)}, u32[]{:S(2)}) collective-permute-start(bf16[256,512]{0,1:T(8,128)(2,1)S(1)} %bitcast.228), channel_id=1, source_target_pairs={{0,2},{1,3},{2,4},{3,5},{4,6},{5,7},{6,8},{7,9},{8,10},{9,11},{10,... | collective-permute-start | bytes 786440 | tf_op jit(solution)/shard_map/ppermute | solution.py:15
  18.0 50.2 %collective-permute-start.3 = (bf16[256,512]{0,1:T(8,128)(2,1)S(1)}, bf16[256,512]{0,1:T(8,128)(2,1)}, u32[]{:S(2)}, u32[]{:S(2)}) collective-permute-start(bf16[256,512]{0,1:T(8,128)(2,1)S(1)} %bitcast.229), channel_id=1, source_target_pairs={{0,3},{1,4},{2,5},{3,6},{4,7},{5,8},{6,9},{7,10},{8,11},{9,12},{10... | collective-permute-start | bytes 786440 | tf_op jit(solution)/shard_map/ppermute | solution.py:15
  21.5 30.2 %collective-permute-start.2 = (bf16[256,512]{1,0:T(8,128)(2,1)}, bf16[256,512]{1,0:T(8,128)(2,1)S(1)}, u32[]{:S(2)}, u32[]{:S(2)}) collective-permute-start(bf16[256,512]{1,0:T(8,128)(2,1)} %bitcast.237), channel_id=1, source_target_pairs={{0,1},{1,2},{2,3},{3,4},{4,5},{5,6},{6,7},{7,8},{8,9},{9,10},{10,1... | collective-permute-start | bytes 786440 | tf_op jit(solution)/shard_map/ppermute | solution.py:15
  23.5 43.5 %collective-permute-start.1 = (bf16[256,512]{1,0:T(8,128)(2,1)}, bf16[256,512]{1,0:T(8,128)(2,1)}, u32[]{:S(2)}, u32[]{:S(2)}) collective-permute-start(bf16[256,512]{1,0:T(8,128)(2,1)} %bitcast.238), channel_id=1, source_target_pairs={{0,2},{1,3},{2,4},{3,5},{4,6},{5,7},{6,8},{7,9},{8,10},{9,11},{10,... | collective-permute-start | bytes 786440 | tf_op jit(solution)/shard_map/ppermute | solution.py:15
  28.7 37.2 %copy-start = (f32[1,256,2560]{1,2,0:T(8,128)}, f32[1,256,2560]{1,2,0:T(8,128)S(1)}, u32[]{:S(2)}) copy-start(f32[1,256,2560]{1,2,0:T(8,128)S(1)} %copy.66) | copy-start | bytes 7864324
  28.7 1.8 copy-start.10
  28.7 23.0 %copy-start.7 = (bf16[1,256,512]{2,1,0:T(8,128)(2,1)S(1)}, bf16[1,256,512]{2,1,0:T(8,128)(2,1)}, u32[]{:S(2)}) copy-start(bf16[1,256,512]{2,1,0:T(8,128)(2,1)} %param.10) | copy-start | bytes 786436
  51.7 11.5 %copy-start.8 = (bf16[256,512]{1,0:T(8,128)(2,1)}, bf16[256,512]{1,0:T(8,128)(2,1)S(1)}, u32[]{:S(2)}) copy-start(bf16[256,512]{1,0:T(8,128)(2,1)S(1)} %collective-permute-done.2) | copy-start | bytes 786436
  51.7 32.4 %collective-permute-start = (bf16[256,512]{1,0:T(8,128)(2,1)S(1)}, bf16[256,512]{1,0:T(8,128)(2,1)}, u32[]{:S(2)}, u32[]{:S(2)}) collective-permute-start(bf16[256,512]{1,0:T(8,128)(2,1)S(1)} %bitcast.239), channel_id=1, source_target_pairs={{0,3},{1,4},{2,5},{3,6},{4,7},{5,8},{6,9},{7,10},{8,11},{9,12},{10... | collective-permute-start | bytes 786440 | tf_op jit(solution)/shard_map/ppermute | solution.py:15
  67.0 19.4 %copy-start.1 = (bf16[4,256,5,128]{1,3,2,0:T(8,128)(2,1)S(1)}, bf16[4,256,5,128]{1,3,2,0:T(8,128)(2,1)}, u32[]{:S(2)}) copy-start(bf16[4,256,5,128]{1,3,2,0:T(8,128)(2,1)} %fusion.35) | copy-start | bytes 3932164
  107.1 1.2 copy-start.5
  154.4 3.7 %copy-start.3 = (f32[4,1024,128]{2,1,0:T(8,128)S(1)}, f32[4,1024,128]{2,1,0:T(8,128)}, u32[]{:S(2)}) copy-start(f32[4,1024,128]{2,1,0:T(8,128)} %get-tuple-element.63) | copy-start | bytes 6291460
  158.4 11.8 %copy-start.4 = (f32[4,1024,128]{2,1,0:T(8,128)S(1)}, f32[4,1024,128]{2,1,0:T(8,128)}, u32[]{:S(2)}) copy-start(f32[4,1024,128]{2,1,0:T(8,128)} %get-tuple-element.62) | copy-start | bytes 6291460
  158.7 39.7 %collective-permute-start.11 = (f32[4,256,128]{2,0,1:T(4,128)S(1)}, f32[4,256,128]{2,0,1:T(4,128)S(1)}, u32[]{:S(2)}, u32[]{:S(2)}) collective-permute-start(f32[4,256,128]{2,0,1:T(4,128)S(1)} %bitcast.236), channel_id=1, source_target_pairs={{3,0},{4,1},{5,2},{6,3},{7,4},{8,5},{9,6},{10,7},{11,8},{12,9},{13... | collective-permute-start | bytes 1572872 | tf_op jit(solution)/shard_map/ppermute | solution.py:15
  166.0 43.8 %collective-permute-start.9 = (f32[4,256,128]{2,0,1:T(4,128)}, f32[4,256,128]{2,0,1:T(4,128)}, u32[]{:S(2)}, u32[]{:S(2)}) collective-permute-start(f32[4,256,128]{2,0,1:T(4,128)} %bitcast.170), channel_id=1, source_target_pairs={{1,0},{2,1},{3,2},{4,3},{5,4},{6,5},{7,6},{8,7},{9,8},{10,9},{11,1... | collective-permute-start | bytes 1572872 | tf_op jit(solution)/shard_map/ppermute | solution.py:15
  168.0 51.1 %collective-permute-start.10 = (f32[4,256,128]{2,0,1:T(4,128)}, f32[4,256,128]{2,0,1:T(4,128)}, u32[]{:S(2)}, u32[]{:S(2)}) collective-permute-start(f32[4,256,128]{2,0,1:T(4,128)} %bitcast.169), channel_id=1, source_target_pairs={{2,0},{3,1},{4,2},{5,3},{6,4},{7,5},{8,6},{9,7},{10,8},{11,9},{12,... | collective-permute-start | bytes 1572872 | tf_op jit(solution)/shard_map/ppermute | solution.py:15
  170.3 30.0 %copy-start.2 = (f32[4,256,5,128]{1,3,2,0:T(8,128)S(1)}, f32[4,256,5,128]{1,3,2,0:T(8,128)}, u32[]{:S(2)}) copy-start(f32[4,256,5,128]{1,3,2,0:T(8,128)} %get-tuple-element.61) | copy-start | bytes 7864324
  170.4 30.0 %copy-start.9 = (f32[2560]{0:T(1024)S(1)}, f32[2560]{0:T(1024)}, u32[]{:S(2)}) copy-start(f32[2560]{0:T(1024)} %param.12) | copy-start | bytes 30724
  173.0 93.9 %collective-permute-start.8 = (f32[4,256,128]{2,0,1:T(4,128)}, f32[4,256,128]{2,0,1:T(4,128)}, u32[]{:S(2)}, u32[]{:S(2)}) collective-permute-start(f32[4,256,128]{2,0,1:T(4,128)} %bitcast.171), channel_id=1, source_target_pairs={{3,0},{4,1},{5,2},{6,3},{7,4},{8,5},{9,6},{10,7},{11,8},{12,9},{13... | collective-permute-start | bytes 1572872 | tf_op jit(solution)/shard_map/ppermute | solution.py:15
  174.9 103.2 %collective-permute-start.6 = (f32[4,256,128]{2,0,1:T(4,128)}, f32[4,256,128]{2,0,1:T(4,128)}, u32[]{:S(2)}, u32[]{:S(2)}) collective-permute-start(f32[4,256,128]{2,0,1:T(4,128)} %bitcast.173), channel_id=1, source_target_pairs={{1,0},{2,1},{3,2},{4,3},{5,4},{6,5},{7,6},{8,7},{9,8},{10,9},{11,1... | collective-permute-start | bytes 1572872 | tf_op jit(solution)/shard_map/ppermute | solution.py:15
  198.4 2.4 copy-start.6
  198.4 87.7 %collective-permute-start.7 = (f32[4,256,128]{2,0,1:T(4,128)S(1)}, f32[4,256,128]{2,0,1:T(4,128)}, u32[]{:S(2)}, u32[]{:S(2)}) collective-permute-start(f32[4,256,128]{2,0,1:T(4,128)S(1)} %bitcast.235), channel_id=1, source_target_pairs={{2,0},{3,1},{4,2},{5,3},{6,4},{7,5},{8,6},{9,7},{10,8},{11,9},{12,... | collective-permute-start | bytes 1572872 | tf_op jit(solution)/shard_map/ppermute | solution.py:15
  (3 other events, 3.7 us)
Sparse Core Ops, SparseCore 0:
  158.3 162.5 all-gather.2
